TPU v7x, 32 devices: a whole 2x2x4 slice. The times are simulated.
32 devices in a mesh: grp: 2 (over x), orient: 16 (over z, y, core).
Axes of the slice: x: 2, y: 2, z: 4, core: 2. Of those that a mesh axis runs over, the one named last changes fastest.
Arguments:
- particles: bfloat16 [2048, 2048], P(('grp', 'orient')), parts along dimension 0, may hold values from -50 to 50
- references: bfloat16 [4096, 2048], P(('grp', 'orient')), parts along dimension 0, may hold values from -4 to 4
- tile_blocks: int32 [32, 6], P('grp'), parts along dimension 0, may hold values from 0 to 7, as said below
- tile_count: int32 [32], P('grp'), parts along dimension 0, may hold values from 1 to 6
- shift_start: int32 [32, 6], P('grp'), parts along dimension 0, may hold values from 1 to 16
Outputs:
- ref_update: float32 [4096, 2048], P(('grp', 'orient')), parts along dimension 0
- weight_sum: float32 [4096], P(('grp', 'orient')), parts along dimension 0
- log_evidence: float32 [2048], P(('grp', 'orient')), parts along dimension 0
There are 2 independent parts, one for each index of `grp`. A program takes and returns all parts, laid end to end along the dimension named above; each array names one. Nothing has to cross between parts.
Inputs may be any that keep to these rules, and one draw needn't show every extreme that they name: `tile_blocks`: in each row the first tile_count entries are distinct particle blocks, and every particle block appears among the used entries of some row.
All inputs are finite; a program needn't handle non-finite values.
Results may differ from a plain program's by a relative error of at most 0.0033.
Values may be sent and summed in bfloat16 or wider, within the bound.
A program may use at most 128 MiB of HBM per device.

v0:
```python
import math
import jax
import jax.numpy as jnp
from jax import lax
from jax.sharding import PartitionSpec as P

K = 2048
NSH = 16
TILE = 128
MOST = 6
very_negative = -1e30


def merged(array, axis, combine):
    everything = jax.tree.map(lambda part: lax.all_gather(part, axis), array)
    leading = jax.tree.map(lambda part: part[0], everything)

    def turn(k, so_far):
        return combine(so_far, jax.tree.map(lambda part: part[k], everything))

    return lax.fori_loop(1, lax.axis_size(axis), turn, leading)


def shift_phases(window_start):
    half_width = K // 2
    freq_index = jnp.arange(half_width, dtype=jnp.int32)
    freq_x = (freq_index % 32).astype(jnp.float32)
    freq_y = (freq_index // 32 - K // 128).astype(jnp.float32)
    grid_index = window_start + jnp.arange(NSH, dtype=jnp.int32)
    delta_x = (grid_index - 16).astype(jnp.float32) * 0.5
    delta_y = (5 * grid_index % 7 - 3).astype(jnp.float32) * 0.5
    angles = (
        2.0
        * math.pi
        / 64.0
        * (delta_x[:, None] * freq_x[None, :] + delta_y[:, None] * freq_y[None, :])
    )
    return (jnp.cos(angles), jnp.sin(angles))


def shifted_images(image_block, window_start):
    cosine_table, sine_table = shift_phases(window_start)
    half_width = K // 2
    real_part = image_block[:, :half_width].astype(jnp.float32)[None]
    imag_part = image_block[:, half_width:].astype(jnp.float32)[None]
    new_real = real_part * cosine_table[:, None, :] - imag_part * sine_table[:, None, :]
    new_imag = real_part * sine_table[:, None, :] + imag_part * cosine_table[:, None, :]
    stacked = jnp.concatenate([new_real, new_imag], axis=2).astype(jnp.bfloat16)
    return stacked.reshape(NSH * image_block.shape[0], K)


def tile_scores(shifted, ref_block, ref_norms):
    products = lax.dot_general(
        shifted, ref_block, (((1,), (1,)), ((), ())), preferred_element_type=jnp.float32
    )
    return (products - 0.5 * ref_norms[None, :]) / math.sqrt(K)


def combine_stats(first_pair, second_pair):
    top_first, sum_first = first_pair
    top_second, sum_second = second_pair
    top_joint = jnp.maximum(top_first, top_second)
    return (
        top_joint,
        sum_first * jnp.exp(top_first - top_joint) + sum_second * jnp.exp(top_second - top_joint),
    )


def body(particles, references, tile_blocks, tile_count, shift_start):
    local_rows = particles.shape[0]
    axis_count = lax.axis_size("orient")
    my_index = lax.axis_index("orient")
    total_rows = local_rows * axis_count
    block_total = total_rows // TILE
    ref_stack = references[None]
    lower_count = tile_count[my_index]
    ref_norms = jnp.sum(ref_stack.astype(jnp.float32) ** 2, axis=2)
    gathered = lax.all_gather(particles, "orient", axis=0, tiled=True)
    by_block = gathered.reshape(TILE, block_total, K)

    def fetch_block(block_id):
        return lax.dynamic_index_in_dim(by_block, block_id, 1, keepdims=False)

    def describe(item_index):
        in_lower = item_index < lower_count
        column = jnp.where(in_lower, my_index, my_index)
        slot_index = jnp.where(in_lower, item_index, item_index - lower_count)
        which_ref = jnp.where(column == my_index, 0, 1)
        block_id = tile_blocks[column, slot_index]
        image_block = fetch_block(block_id)
        shifted = shifted_images(image_block, shift_start[column, slot_index])
        return (which_ref, block_id, shifted)

    def first_pass(item_index, loop_state):
        score_store, running_top, running_sum = loop_state
        which_ref, block_id, shifted = describe(item_index)
        ref_block = lax.dynamic_index_in_dim(ref_stack, which_ref, 0, keepdims=False)
        norms = lax.dynamic_index_in_dim(ref_norms, which_ref, 0, keepdims=False)
        scores = tile_scores(shifted, ref_block, norms)
        by_particle = scores.reshape(NSH, TILE, TILE)
        tile_top = jnp.max(by_particle, axis=(0, 2))
        old_top = lax.dynamic_index_in_dim(running_top, block_id, 1, keepdims=False)
        old_sum = lax.dynamic_index_in_dim(running_sum, block_id, 1, keepdims=False)
        new_top = jnp.maximum(old_top, tile_top)
        tile_sum = jnp.sum(jnp.exp(by_particle - new_top[None, :, None]), axis=(0, 2))
        new_sum = old_sum * jnp.exp(old_top - new_top) + tile_sum
        running_top = lax.dynamic_update_index_in_dim(running_top, new_top, block_id, 1)
        running_sum = lax.dynamic_update_index_in_dim(running_sum, new_sum, block_id, 1)
        score_store = lax.dynamic_update_index_in_dim(score_store, scores, item_index, 0)
        return (score_store, running_top, running_sum)

    start_state = (
        jnp.zeros((MOST, NSH * TILE, TILE), jnp.float32),
        jnp.full((TILE, block_total), very_negative, jnp.float32),
        jnp.zeros((TILE, block_total), jnp.float32),
    )
    score_store, running_top, running_sum = lax.fori_loop(0, lower_count, first_pass, start_state)
    global_top, global_sum = merged((running_top, running_sum), "orient", combine_stats)

    def second_pass(item_index, loop_state):
        update_acc, weight_acc = loop_state
        which_ref, block_id, shifted = describe(item_index)
        particle_top = lax.dynamic_index_in_dim(global_top, block_id, 1, keepdims=False)
        particle_sum = lax.dynamic_index_in_dim(global_sum, block_id, 1, keepdims=False)
        item_scores = lax.dynamic_index_in_dim(score_store, item_index, 0, keepdims=False).reshape(
            NSH, TILE, TILE
        )
        weights = (
            jnp.exp(item_scores - particle_top[None, :, None]) / particle_sum[None, :, None]
        ).astype(jnp.bfloat16)
        weights = weights.reshape(NSH * TILE, TILE)
        update = lax.dot_general(
            weights, shifted, (((0,), (0,)), ((), ())), preferred_element_type=jnp.float32
        )
        weight_total = jnp.sum(weights.astype(jnp.float32), axis=0)
        current = lax.dynamic_index_in_dim(update_acc, which_ref, 0, keepdims=False)
        update_acc = lax.dynamic_update_index_in_dim(update_acc, current + update, which_ref, 0)
        current_weight = lax.dynamic_index_in_dim(weight_acc, which_ref, 0, keepdims=False)
        weight_acc = lax.dynamic_update_index_in_dim(
            weight_acc, current_weight + weight_total, which_ref, 0
        )
        return (update_acc, weight_acc)

    stack_depth = ref_stack.shape[0]
    back_state = (
        jnp.zeros((stack_depth, TILE, K), jnp.float32),
        jnp.zeros((stack_depth, TILE), jnp.float32),
    )
    update_acc, weight_acc = lax.fori_loop(0, lower_count, second_pass, back_state)
    ref_update = update_acc[0]
    weight_sum = weight_acc[0]
    evidence = (global_top + jnp.log(global_sum)).reshape(total_rows)
    log_evidence = lax.dynamic_slice_in_dim(evidence, my_index * local_rows, local_rows, 0)
    return (ref_update, weight_sum, log_evidence)


def solution(mesh):
    in_specs = (
        P(("grp", "orient"), None),
        P(("grp", "orient"), None),
        P("grp", None),
        P("grp"),
        P("grp", None),
    )
    out_specs = (P(("grp", "orient"), None), P(("grp", "orient")), P(("grp", "orient")))
    return jax.shard_map(body, mesh=mesh, in_specs=in_specs, out_specs=out_specs, check_vma=False)
```

profile of v0, /device:TPU:30, one launch (start us, length us, event | category | flops | bytes accessed | tf_op | source)
XLA Modules:
  0.0 364.0 jit_solution(5189252617112790068)
XLA Ops:
  7.9 1.2 dynamic_slice.113
  9.1 1.2 multiply_reduce_fusion
  10.4 48.7 %all-gather.4.cloned.1.call-done = bf16[1024,2048]{1,0:T(8,128)(2,1)} async-done(((bf16[64,2048]{1,0:T(8,128)(2,1)}), bf16[1024,2048]{1,0:T(8,128)(2,1)}) %all-gather.4.cloned.1.call-update) | async-done | bytes 4194320 | tf_op jit(solution)/shard_map/all_gather | solution.py:78
  59.1 6.6 %copy.16 = bf16[128,8,2048]{2,0,1:T(8,128)(2,1)} copy(bf16[128,8,2048]{2,1,0:T(8,128)(2,1)} %bitcast.141) | data formatting | bytes 8388608 | tf_op jit(solution)/shard_map/while | solution.py:117
  65.6 3.4 broadcast_in_dim.45
  69.1 127.2 %while.49 = (s32[]{:T(128)}, f32[6,2048,128]{1,2,0:T(8,128)}, f32[128,8]{0,1:T(8,128)S(1)}, f32[128,8]{0,1:T(8,128)S(1)}, s32[]{:T(128)}, /*index=5*/s32[16,6]{0...) while((s32[]{:T(128)}, f32[6,2048,128]{1,2,0:T(8,128)}, ...), condition=%wide.region_6.7_spmd, body=%wide.region_1.6_spmd.sunk | while | flops 1108950784 | bytes 25503828 | solution.py:117
  71.0 1.3 dynamic_slice.157
  74.2 1.1 dynamic-slice_bitcast_fusion.4
  75.4 1.3 dynamic_slice.156
  77.6 4.8 %subtract_convert_fusion.4 = (bf16[16,128,1024]{2,1,0:T(8,128)(2,1)}, bf16[16,128,1024]{2,1,0:T(8,128)(2,1)}) fusion(f32[16,1024]{1,0:T(8,128)S(1)} %get-tuple-element.877, f32[128,1024]{1,0:T(8,128)S(1)} %get-tuple-element.878, f32[16,1024]{1,0:T(8,128)S(1)} %get-tuple-element.879, f32[128,1024]{1,0:T(8,128)S(1)} %get-tuple-element.880), kind=kLoop, calls=%fused_computation.5.clone.1 | loop fusion | flops 16777216 | bytes 9568256 | tf_op jit(solution)/shard_map/convert.3
  82.4 7.3 %bitcast_dynamic-update-slice_fusion.2 = (f32[6,2048,128]{1,2,0:T(8,128)}, f32[2048,128]{0,1:T(8,128)S(1)}) fusion(f32[6,2048,128]{1,2,0:T(8,128)} %get-tuple-element.934, s32[]{:T(128)S(6)} %select_n.243, f32[128]{0:T(128)S(1)} %multiply_bitcast_fusion.2, bf16[1,128,2048]{2,1,0:T(8,128)(2,1)S(1)} %get-tuple-element.958, ...), kind=kOutput, calls=%fused_computation.8.clone.1 | convolution fusion | flops 1091043328 | bytes 11010564 | tf_op jit(solution)/shard_map/while/body/dot_general | solution.py:53
  92.1 1.3 dynamic_slice.157
  96.4 1.3 dynamic_slice.156
  98.7 4.8 %subtract_convert_fusion.4 = (bf16[16,128,1024]{2,1,0:T(8,128)(2,1)}, bf16[16,128,1024]{2,1,0:T(8,128)(2,1)}) fusion(f32[16,1024]{1,0:T(8,128)S(1)} %get-tuple-element.877, f32[128,1024]{1,0:T(8,128)S(1)} %get-tuple-element.878, f32[16,1024]{1,0:T(8,128)S(1)} %get-tuple-element.879, f32[128,1024]{1,0:T(8,128)S(1)} %get-tuple-element.880), kind=kLoop, calls=%fused_computation.5.clone.1 | loop fusion | flops 16777216 | bytes 9568256 | tf_op jit(solution)/shard_map/convert.3
  103.5 7.4 %bitcast_dynamic-update-slice_fusion.2 = (f32[6,2048,128]{1,2,0:T(8,128)}, f32[2048,128]{0,1:T(8,128)S(1)}) fusion(f32[6,2048,128]{1,2,0:T(8,128)} %get-tuple-element.934, s32[]{:T(128)S(6)} %select_n.243, f32[128]{0:T(128)S(1)} %multiply_bitcast_fusion.2, bf16[1,128,2048]{2,1,0:T(8,128)(2,1)S(1)} %get-tuple-element.958, ...), kind=kOutput, calls=%fused_computation.8.clone.1 | convolution fusion | flops 1091043328 | bytes 11010564 | tf_op jit(solution)/shard_map/while/body/dot_general | solution.py:53
  113.2 1.3 dynamic_slice.157
  117.6 1.3 dynamic_slice.156
  119.8 4.8 %subtract_convert_fusion.4 = (bf16[16,128,1024]{2,1,0:T(8,128)(2,1)}, bf16[16,128,1024]{2,1,0:T(8,128)(2,1)}) fusion(f32[16,1024]{1,0:T(8,128)S(1)} %get-tuple-element.877, f32[128,1024]{1,0:T(8,128)S(1)} %get-tuple-element.878, f32[16,1024]{1,0:T(8,128)S(1)} %get-tuple-element.879, f32[128,1024]{1,0:T(8,128)S(1)} %get-tuple-element.880), kind=kLoop, calls=%fused_computation.5.clone.1 | loop fusion | flops 16777216 | bytes 9568256 | tf_op jit(solution)/shard_map/convert.3
  124.6 7.4 %bitcast_dynamic-update-slice_fusion.2 = (f32[6,2048,128]{1,2,0:T(8,128)}, f32[2048,128]{0,1:T(8,128)S(1)}) fusion(f32[6,2048,128]{1,2,0:T(8,128)} %get-tuple-element.934, s32[]{:T(128)S(6)} %select_n.243, f32[128]{0:T(128)S(1)} %multiply_bitcast_fusion.2, bf16[1,128,2048]{2,1,0:T(8,128)(2,1)S(1)} %get-tuple-element.958, ...), kind=kOutput, calls=%fused_computation.8.clone.1 | convolution fusion | flops 1091043328 | bytes 11010564 | tf_op jit(solution)/shard_map/while/body/dot_general | solution.py:53
  134.3 1.3 dynamic_slice.157
  138.6 1.3 dynamic_slice.156
  140.9 4.8 %subtract_convert_fusion.4 = (bf16[16,128,1024]{2,1,0:T(8,128)(2,1)}, bf16[16,128,1024]{2,1,0:T(8,128)(2,1)}) fusion(f32[16,1024]{1,0:T(8,128)S(1)} %get-tuple-element.877, f32[128,1024]{1,0:T(8,128)S(1)} %get-tuple-element.878, f32[16,1024]{1,0:T(8,128)S(1)} %get-tuple-element.879, f32[128,1024]{1,0:T(8,128)S(1)} %get-tuple-element.880), kind=kLoop, calls=%fused_computation.5.clone.1 | loop fusion | flops 16777216 | bytes 9568256 | tf_op jit(solution)/shard_map/convert.3
  145.7 7.3 %bitcast_dynamic-update-slice_fusion.2 = (f32[6,2048,128]{1,2,0:T(8,128)}, f32[2048,128]{0,1:T(8,128)S(1)}) fusion(f32[6,2048,128]{1,2,0:T(8,128)} %get-tuple-element.934, s32[]{:T(128)S(6)} %select_n.243, f32[128]{0:T(128)S(1)} %multiply_bitcast_fusion.2, bf16[1,128,2048]{2,1,0:T(8,128)(2,1)S(1)} %get-tuple-element.958, ...), kind=kOutput, calls=%fused_computation.8.clone.1 | convolution fusion | flops 1091043328 | bytes 11010564 | tf_op jit(solution)/shard_map/while/body/dot_general | solution.py:53
  155.4 1.3 dynamic_slice.157
  159.7 1.3 dynamic_slice.156
  162.0 4.8 %subtract_convert_fusion.4 = (bf16[16,128,1024]{2,1,0:T(8,128)(2,1)}, bf16[16,128,1024]{2,1,0:T(8,128)(2,1)}) fusion(f32[16,1024]{1,0:T(8,128)S(1)} %get-tuple-element.877, f32[128,1024]{1,0:T(8,128)S(1)} %get-tuple-element.878, f32[16,1024]{1,0:T(8,128)S(1)} %get-tuple-element.879, f32[128,1024]{1,0:T(8,128)S(1)} %get-tuple-element.880), kind=kLoop, calls=%fused_computation.5.clone.1 | loop fusion | flops 16777216 | bytes 9568256 | tf_op jit(solution)/shard_map/convert.3
  166.8 7.4 %bitcast_dynamic-update-slice_fusion.2 = (f32[6,2048,128]{1,2,0:T(8,128)}, f32[2048,128]{0,1:T(8,128)S(1)}) fusion(f32[6,2048,128]{1,2,0:T(8,128)} %get-tuple-element.934, s32[]{:T(128)S(6)} %select_n.243, f32[128]{0:T(128)S(1)} %multiply_bitcast_fusion.2, bf16[1,128,2048]{2,1,0:T(8,128)(2,1)S(1)} %get-tuple-element.958, ...), kind=kOutput, calls=%fused_computation.8.clone.1 | convolution fusion | flops 1091043328 | bytes 11010564 | tf_op jit(solution)/shard_map/while/body/dot_general | solution.py:53
  176.5 1.3 dynamic_slice.157
  180.8 1.3 dynamic_slice.156
  183.0 4.8 %subtract_convert_fusion.4 = (bf16[16,128,1024]{2,1,0:T(8,128)(2,1)}, bf16[16,128,1024]{2,1,0:T(8,128)(2,1)}) fusion(f32[16,1024]{1,0:T(8,128)S(1)} %get-tuple-element.877, f32[128,1024]{1,0:T(8,128)S(1)} %get-tuple-element.878, f32[16,1024]{1,0:T(8,128)S(1)} %get-tuple-element.879, f32[128,1024]{1,0:T(8,128)S(1)} %get-tuple-element.880), kind=kLoop, calls=%fused_computation.5.clone.1 | loop fusion | flops 16777216 | bytes 9568256 | tf_op jit(solution)/shard_map/convert.3
  187.8 7.4 %bitcast_dynamic-update-slice_fusion.2 = (f32[6,2048,128]{1,2,0:T(8,128)}, f32[2048,128]{0,1:T(8,128)S(1)}) fusion(f32[6,2048,128]{1,2,0:T(8,128)} %get-tuple-element.934, s32[]{:T(128)S(6)} %select_n.243, f32[128]{0:T(128)S(1)} %multiply_bitcast_fusion.2, bf16[1,128,2048]{2,1,0:T(8,128)(2,1)S(1)} %get-tuple-element.958, ...), kind=kOutput, calls=%fused_computation.8.clone.1 | convolution fusion | flops 1091043328 | bytes 11010564 | tf_op jit(solution)/shard_map/while/body/dot_general | solution.py:53
  196.3 16.7 %all-gather = f32[2048,8]{0,1:T(8,128)S(1)} all-gather(f32[128,8]{0,1:T(8,128)S(1)} %get-tuple-element.540), channel_id=2, replica_groups=mesh['grp'=2,'orient'=16] {'orient'}, dimensions={0}, use_global_device_ids=true | all-gather | bytes 69632 | tf_op jit(solution)/shard_map/all_gather | solution.py:15
  212.9 19.8 %all-gather.1 = f32[2048,8]{0,1:T(8,128)S(1)} all-gather(f32[128,8]{0,1:T(8,128)S(1)} %get-tuple-element.541), channel_id=3, replica_groups=mesh['grp'=2,'orient'=16] {'orient'}, dimensions={0}, use_global_device_ids=true | all-gather | bytes 69632 | tf_op jit(solution)/shard_map/all_gather | solution.py:15
  233.7 122.5 %while.51 = (s32[]{:T(128)}, f32[1,128,2048]{2,1,0:T(8,128)S(1)}, f32[1,128]{1,0:T(1,128)S(1)}, s32[]{:T(128)}, f32[6,2048,128]{1,2,0:T(8,128)}, /*index=5*/s32[...) while((s32[]{:T(128)}, f32[1,128,2048]{2,1,0:T(8,128)S(1)}, ...), condition=%wide.region_11.12_spmd, body=%wide.region_9.11_spmd.sunk | while | flops 1109998848 | bytes 29153852 | solution.py:149
  235.7 1.3 dynamic_slice.163
  240.0 1.3 dynamic_slice.162
  242.2 4.8 %subtract_convert_fusion.5 = (bf16[16,128,1024]{2,1,0:T(8,128)(2,1)}, bf16[16,128,1024]{2,1,0:T(8,128)(2,1)}) fusion(f32[16,1024]{1,0:T(8,128)S(1)} %get-tuple-element.909, f32[128,1024]{1,0:T(8,128)S(1)} %get-tuple-element.910, f32[16,1024]{1,0:T(8,128)S(1)} %get-tuple-element.911, f32[128,1024]{1,0:T(8,128)S(1)} %get-tuple-element.912), kind=kLoop, calls=%fused_computation.57.clone.1 | loop fusion | flops 16777216 | bytes 9568256 | tf_op jit(solution)/shard_map/convert.4
  247.0 1.3 constant_dynamic-slice_fusion.6
  248.7 4.6 %fusion.84 = f32[1,128,2048]{2,1,0:T(8,128)S(1)} fusion(bf16[16,128,1024]{2,1,0:T(8,128)(2,1)} %get-tuple-element.913, bf16[16,128,1024]{2,1,0:T(8,128)(2,1)} %get-tuple-element.914, f32[1,128,2048]{2,1,0:T(8,128)S(1)} %get-tuple-element.1005, f32[16,128,128]{2,1,0:T(8,128)S(1)} %bitcast.140, f32[128]{0:T(128)S(1)} %get-tuple-element.915, ...), kind=kOutput, calls=%fused_computation.60.clone.1 | convolution fusion | flops 1091567616 | bytes 11535360 | tf_op jit(solution)/shard_map/while/body/dot_general | solution.py:132
  256.0 1.3 dynamic_slice.163
  260.3 1.3 dynamic_slice.162
  262.6 4.8 %subtract_convert_fusion.5 = (bf16[16,128,1024]{2,1,0:T(8,128)(2,1)}, bf16[16,128,1024]{2,1,0:T(8,128)(2,1)}) fusion(f32[16,1024]{1,0:T(8,128)S(1)} %get-tuple-element.909, f32[128,1024]{1,0:T(8,128)S(1)} %get-tuple-element.910, f32[16,1024]{1,0:T(8,128)S(1)} %get-tuple-element.911, f32[128,1024]{1,0:T(8,128)S(1)} %get-tuple-element.912), kind=kLoop, calls=%fused_computation.57.clone.1 | loop fusion | flops 16777216 | bytes 9568256 | tf_op jit(solution)/shard_map/convert.4
  267.3 1.3 constant_dynamic-slice_fusion.6
  269.0 4.6 %fusion.84 = f32[1,128,2048]{2,1,0:T(8,128)S(1)} fusion(bf16[16,128,1024]{2,1,0:T(8,128)(2,1)} %get-tuple-element.913, bf16[16,128,1024]{2,1,0:T(8,128)(2,1)} %get-tuple-element.914, f32[1,128,2048]{2,1,0:T(8,128)S(1)} %get-tuple-element.1005, f32[16,128,128]{2,1,0:T(8,128)S(1)} %bitcast.140, f32[128]{0:T(128)S(1)} %get-tuple-element.915, ...), kind=kOutput, calls=%fused_computation.60.clone.1 | convolution fusion | flops 1091567616 | bytes 11535360 | tf_op jit(solution)/shard_map/while/body/dot_general | solution.py:132
  276.3 1.3 dynamic_slice.163
  280.6 1.3 dynamic_slice.162
  282.9 4.8 %subtract_convert_fusion.5 = (bf16[16,128,1024]{2,1,0:T(8,128)(2,1)}, bf16[16,128,1024]{2,1,0:T(8,128)(2,1)}) fusion(f32[16,1024]{1,0:T(8,128)S(1)} %get-tuple-element.909, f32[128,1024]{1,0:T(8,128)S(1)} %get-tuple-element.910, f32[16,1024]{1,0:T(8,128)S(1)} %get-tuple-element.911, f32[128,1024]{1,0:T(8,128)S(1)} %get-tuple-element.912), kind=kLoop, calls=%fused_computation.57.clone.1 | loop fusion | flops 16777216 | bytes 9568256 | tf_op jit(solution)/shard_map/convert.4
  287.7 1.3 constant_dynamic-slice_fusion.6
  289.3 4.6 %fusion.84 = f32[1,128,2048]{2,1,0:T(8,128)S(1)} fusion(bf16[16,128,1024]{2,1,0:T(8,128)(2,1)} %get-tuple-element.913, bf16[16,128,1024]{2,1,0:T(8,128)(2,1)} %get-tuple-element.914, f32[1,128,2048]{2,1,0:T(8,128)S(1)} %get-tuple-element.1005, f32[16,128,128]{2,1,0:T(8,128)S(1)} %bitcast.140, f32[128]{0:T(128)S(1)} %get-tuple-element.915, ...), kind=kOutput, calls=%fused_computation.60.clone.1 | convolution fusion | flops 1091567616 | bytes 11535360 | tf_op jit(solution)/shard_map/while/body/dot_general | solution.py:132
  296.6 1.3 dynamic_slice.163
  300.9 1.3 dynamic_slice.162
  303.2 4.8 %subtract_convert_fusion.5 = (bf16[16,128,1024]{2,1,0:T(8,128)(2,1)}, bf16[16,128,1024]{2,1,0:T(8,128)(2,1)}) fusion(f32[16,1024]{1,0:T(8,128)S(1)} %get-tuple-element.909, f32[128,1024]{1,0:T(8,128)S(1)} %get-tuple-element.910, f32[16,1024]{1,0:T(8,128)S(1)} %get-tuple-element.911, f32[128,1024]{1,0:T(8,128)S(1)} %get-tuple-element.912), kind=kLoop, calls=%fused_computation.57.clone.1 | loop fusion | flops 16777216 | bytes 9568256 | tf_op jit(solution)/shard_map/convert.4
  308.0 1.3 constant_dynamic-slice_fusion.6
  309.6 4.6 %fusion.84 = f32[1,128,2048]{2,1,0:T(8,128)S(1)} fusion(bf16[16,128,1024]{2,1,0:T(8,128)(2,1)} %get-tuple-element.913, bf16[16,128,1024]{2,1,0:T(8,128)(2,1)} %get-tuple-element.914, f32[1,128,2048]{2,1,0:T(8,128)S(1)} %get-tuple-element.1005, f32[16,128,128]{2,1,0:T(8,128)S(1)} %bitcast.140, f32[128]{0:T(128)S(1)} %get-tuple-element.915, ...), kind=kOutput, calls=%fused_computation.60.clone.1 | convolution fusion | flops 1091567616 | bytes 11535360 | tf_op jit(solution)/shard_map/while/body/dot_general | solution.py:132
  316.9 1.3 dynamic_slice.163
  321.2 1.3 dynamic_slice.162
  323.5 4.8 %subtract_convert_fusion.5 = (bf16[16,128,1024]{2,1,0:T(8,128)(2,1)}, bf16[16,128,1024]{2,1,0:T(8,128)(2,1)}) fusion(f32[16,1024]{1,0:T(8,128)S(1)} %get-tuple-element.909, f32[128,1024]{1,0:T(8,128)S(1)} %get-tuple-element.910, f32[16,1024]{1,0:T(8,128)S(1)} %get-tuple-element.911, f32[128,1024]{1,0:T(8,128)S(1)} %get-tuple-element.912), kind=kLoop, calls=%fused_computation.57.clone.1 | loop fusion | flops 16777216 | bytes 9568256 | tf_op jit(solution)/shard_map/convert.4
  328.3 1.3 constant_dynamic-slice_fusion.6
  329.9 4.6 %fusion.84 = f32[1,128,2048]{2,1,0:T(8,128)S(1)} fusion(bf16[16,128,1024]{2,1,0:T(8,128)(2,1)} %get-tuple-element.913, bf16[16,128,1024]{2,1,0:T(8,128)(2,1)} %get-tuple-element.914, f32[1,128,2048]{2,1,0:T(8,128)S(1)} %get-tuple-element.1005, f32[16,128,128]{2,1,0:T(8,128)S(1)} %bitcast.140, f32[128]{0:T(128)S(1)} %get-tuple-element.915, ...), kind=kOutput, calls=%fused_computation.60.clone.1 | convolution fusion | flops 1091567616 | bytes 11535360 | tf_op jit(solution)/shard_map/while/body/dot_general | solution.py:132
  337.2 1.3 dynamic_slice.163
  341.5 1.3 dynamic_slice.162
  343.8 4.8 %subtract_convert_fusion.5 = (bf16[16,128,1024]{2,1,0:T(8,128)(2,1)}, bf16[16,128,1024]{2,1,0:T(8,128)(2,1)}) fusion(f32[16,1024]{1,0:T(8,128)S(1)} %get-tuple-element.909, f32[128,1024]{1,0:T(8,128)S(1)} %get-tuple-element.910, f32[16,1024]{1,0:T(8,128)S(1)} %get-tuple-element.911, f32[128,1024]{1,0:T(8,128)S(1)} %get-tuple-element.912), kind=kLoop, calls=%fused_computation.57.clone.1 | loop fusion | flops 16777216 | bytes 9568256 | tf_op jit(solution)/shard_map/convert.4
  348.6 1.3 constant_dynamic-slice_fusion.6
  350.2 4.6 %fusion.84 = f32[1,128,2048]{2,1,0:T(8,128)S(1)} fusion(bf16[16,128,1024]{2,1,0:T(8,128)(2,1)} %get-tuple-element.913, bf16[16,128,1024]{2,1,0:T(8,128)(2,1)} %get-tuple-element.914, f32[1,128,2048]{2,1,0:T(8,128)S(1)} %get-tuple-element.1005, f32[16,128,128]{2,1,0:T(8,128)S(1)} %bitcast.140, f32[128]{0:T(128)S(1)} %get-tuple-element.915, ...), kind=kOutput, calls=%fused_computation.60.clone.1 | convolution fusion | flops 1091567616 | bytes 11535360 | tf_op jit(solution)/shard_map/while/body/dot_general | solution.py:132
  (189 shorter events, 36.1 us)
Async XLA Ops:
  7.2 51.9 %all-gather.4.cloned.1.call-start = ((), (), s32[]{:S(2)}) async-start(), calls=%async_computation | async-start | bytes 4456448 | tf_op jit(solution)/shard_map/all_gather | solution.py:78
  59.1 10.0 %copy-start.1 = (bf16[128,2048]{1,0:T(8,128)(2,1)S(1)}, bf16[128,2048]{1,0:T(8,128)(2,1)}, u32[]{:S(2)}) copy-start(bf16[128,2048]{1,0:T(8,128)(2,1)} %param.12) | copy-start | bytes 1572868
  356.2 1.0 copy-start
  356.2 1.0 copy-start.2
Sparse Core Ops, SparseCore 0:
  10.1 48.8 all-gather.3
where the time goes:
time: 366 us; the launch traced here: 364 us
  other arithmetic  77.9 us (21%)
  matrix products  71.5 us (20%)
  local copies, waits for them, and re-layouts  66.5 us (18%)
  waiting for transfers between devices  49.4 us (13%)
  loops' own time  48.1 us (13%)
  blocking collectives  36.5 us (10%)
  between operations  14.1 us (4%)
    another operation x12, other arithmetic  57.5 us
    all_gather x1, waiting for transfers between devices, body(): gathered = lax.all_gather(particles, 'orient', axis=0, tiled=True)  48.7 us
    dot_general x6, matrix products, tile_scores(): lax.dot_general(shifted, ref_block, (((1,), (1,)), ((), ())), preferred_e...  44.2 us
    all_gather x2, blocking collectives, merged(): everything = jax.tree.map(lambda part: lax.all_gather(part, axis), array)  36.5 us
    dot_general x6, matrix products, second_pass(): lax.dot_general(weights, shifted, (((0,), (0,)), ((), ())), preferred_ele...  27.3 us
    another operation x1, loops' own time, body(): lax.fori_loop(0, lower_count, second_pass, back_state)  24 us
    another operation x1, loops' own time, body(): lax.fori_loop(0, lower_count, first_pass, start_state)  23.8 us
    dynamic_slice x12, local copies, waits for them, and re-layouts, describe(): block_id = tile_blocks[column, slot_index]  15.4 us
  transfers between devices with their start and end apart: 1, of which 1 were waited for; matrix products, arithmetic and copies ran while one was open for 1% of the time, Pallas kernels for 0%

commit v1 on v0

--- a/solution.py
+++ b/solution.py
@@ -75,7 +75,15 @@
     ref_stack = references[None]
     lower_count = tile_count[my_index]
     ref_norms = jnp.sum(ref_stack.astype(jnp.float32) ** 2, axis=2)
-    gathered = lax.all_gather(particles, "orient", axis=0, tiled=True)
+    ways, here, hop = (lax.axis_size("orient"), lax.axis_index("orient"), particles.shape[0])
+    line, have = (particles, 1)
+    while have < ways:
+        line = jnp.concatenate(
+            [line, lax.ppermute(line, "orient", [(d, (d - have) % ways) for d in range(ways)])],
+            axis=0,
+        )
+        have = 2 * have
+    gathered = jnp.roll(line, here * hop, axis=0)
     by_block = gathered.reshape(TILE, block_total, K)
 
     def fetch_block(block_id):

time: 366 us -> 441 us (1.20)
  waiting for transfers between devices: 49.4 us -> 129 us
  between operations: 14.1 us -> 0.84 us
  other arithmetic: 77.9 us -> 83.2 us
    ppermute x0 -> x4, waiting for transfers between devices: none -> 129 us  [body(): lax.ppermute(line, 'orient', [(d, (d - have) % ways) for d in range(ways)])]
    all_gather x1 -> x0, waiting for transfers between devices: 48.7 us -> none  [body(): gathered = lax.all_gather(particles, 'orient', axis=0, tiled=True)]
    concatenate x0 -> x3, other arithmetic: none -> 4.71 us  [body(): jnp.concatenate([line, lax.ppermute(line, 'orient', [(d, (d - have) % way...]
  transfers between devices with their start and end apart: 1 -> 4, of which waited for: 1 -> 4; matrix products, arithmetic and copies ran while one was open for 1% -> 1% of each run, Pallas kernels for 0% -> 0%
where the time goes in v1:
time: 441 us; the launch traced here: 438 us
  waiting for transfers between devices  129 us (29%)
  other arithmetic  83.2 us (19%)
  matrix products  71.5 us (16%)
  local copies, waits for them, and re-layouts  68.3 us (15%)
  loops' own time  46.6 us (11%)
  blocking collectives  36.5 us (8%)
    ppermute x4, waiting for transfers between devices, body(): lax.ppermute(line, 'orient', [(d, (d - have) % ways) for d in range(ways)])  129 us
    another operation x12, other arithmetic  57.8 us
    dot_general x6, matrix products, tile_scores(): lax.dot_general(shifted, ref_block, (((1,), (1,)), ((), ())), preferred_e...  44.2 us
    all_gather x2, blocking collectives, merged(): everything = jax.tree.map(lambda part: lax.all_gather(part, axis), array)  36.5 us
    dot_general x6, matrix products, second_pass(): lax.dot_general(weights, shifted, (((0,), (0,)), ((), ())), preferred_ele...  27.3 us
    another operation x1, loops' own time, body(): lax.fori_loop(0, lower_count, second_pass, back_state)  23.3 us
    another operation x1, loops' own time, body(): lax.fori_loop(0, lower_count, first_pass, start_state)  23 us
    dynamic_slice x12, local copies, waits for them, and re-layouts, describe(): block_id = tile_blocks[column, slot_index]  15.3 us
  transfers between devices with their start and end apart: 4, of which 4 were waited for; matrix products, arithmetic and copies ran while one was open for 1% of the time, Pallas kernels for 0%

profile of v1, /device:TPU:30, one launch (start us, length us, event | category | flops | bytes accessed | tf_op | source)
XLA Modules:
  0.0 438.1 jit_solution(13681935178760060273)
XLA Ops:
  0.7 4.2 collective-permute-done
  6.0 1.4 collective-permute-start.1
  7.4 12.8 %collective-permute-done.1 = bf16[128,2048]{1,0:T(8,128)(2,1)S(1)} collective-permute-done((bf16[128,2048]{1,0:T(8,128)(2,1)S(1)}, bf16[128,2048]{1,0:T(8,128)(2,1)S(1)}, u32[]{:S(2)}, u32[]{:S(2)}) %collective-permute-start.1) | collective-permute-done | bytes 524320 | tf_op jit(solution)/shard_map/ppermute | solution.py:82
  21.9 25.2 %collective-permute-done.2 = bf16[256,2048]{1,0:T(8,128)(2,1)S(1)} collective-permute-done((bf16[256,2048]{1,0:T(8,128)(2,1)S(1)}, bf16[256,2048]{1,0:T(8,128)(2,1)S(1)}, u32[]{:S(2)}, u32[]{:S(2)}) %collective-permute-start.2) | collective-permute-done | bytes 1048608 | tf_op jit(solution)/shard_map/ppermute | solution.py:82
  47.1 2.4 pad_maximum_fusion
  49.9 1.3 dynamic_slice.117
  55.5 86.7 %collective-permute-done.3 = bf16[512,2048]{1,0:T(8,128)(2,1)S(1)} collective-permute-done((bf16[512,2048]{1,0:T(8,128)(2,1)}, bf16[512,2048]{1,0:T(8,128)(2,1)S(1)}, u32[]{:S(2)}, u32[]{:S(2)}) %collective-permute-start.3) | collective-permute-done | bytes 2097184 | tf_op jit(solution)/shard_map/ppermute | solution.py:82
  143.3 4.3 copy.16
  147.7 3.4 broadcast_in_dim.45
  151.1 126.6 %while.49 = (s32[]{:T(128)}, f32[6,2048,128]{1,2,0:T(8,128)}, f32[128,8]{0,1:T(8,128)S(1)}, f32[128,8]{0,1:T(8,128)S(1)}, s32[]{:T(128)}, /*index=5*/s32[16,6]{0...) while((s32[]{:T(128)}, f32[6,2048,128]{1,2,0:T(8,128)}, ...), condition=%wide.region_6.7_spmd, body=%wide.region_1.6_spmd.sunk | while | flops 1108950784 | bytes 25503828 | solution.py:125
  152.9 1.3 dynamic_slice.163
  157.3 1.3 dynamic_slice.162
  159.6 4.8 %subtract_convert_fusion.4 = (bf16[16,128,1024]{2,1,0:T(8,128)(2,1)}, bf16[16,128,1024]{2,1,0:T(8,128)(2,1)}) fusion(f32[16,1024]{1,0:T(8,128)S(1)} %get-tuple-element.877, f32[128,1024]{1,0:T(8,128)S(1)} %get-tuple-element.878, f32[16,1024]{1,0:T(8,128)S(1)} %get-tuple-element.879, f32[128,1024]{1,0:T(8,128)S(1)} %get-tuple-element.880), kind=kLoop, calls=%fused_computation.5.clone.1 | loop fusion | flops 16777216 | bytes 9568256 | tf_op jit(solution)/shard_map/convert.3
  164.4 7.3 %bitcast_dynamic-update-slice_fusion.2 = (f32[6,2048,128]{1,2,0:T(8,128)}, f32[2048,128]{0,1:T(8,128)S(1)}) fusion(f32[6,2048,128]{1,2,0:T(8,128)} %get-tuple-element.934, s32[]{:T(128)S(6)} %select_n.258, f32[128]{0:T(128)S(1)} %multiply_bitcast_fusion.2, bf16[1,128,2048]{2,1,0:T(8,128)(2,1)S(1)} %get-tuple-element.958, ...), kind=kOutput, calls=%fused_computation.8.clone.1 | convolution fusion | flops 1091043328 | bytes 11010564 | tf_op jit(solution)/shard_map/while/body/dot_general | solution.py:53
  173.8 1.3 dynamic_slice.163
  178.3 1.3 dynamic_slice.162
  180.5 4.8 %subtract_convert_fusion.4 = (bf16[16,128,1024]{2,1,0:T(8,128)(2,1)}, bf16[16,128,1024]{2,1,0:T(8,128)(2,1)}) fusion(f32[16,1024]{1,0:T(8,128)S(1)} %get-tuple-element.877, f32[128,1024]{1,0:T(8,128)S(1)} %get-tuple-element.878, f32[16,1024]{1,0:T(8,128)S(1)} %get-tuple-element.879, f32[128,1024]{1,0:T(8,128)S(1)} %get-tuple-element.880), kind=kLoop, calls=%fused_computation.5.clone.1 | loop fusion | flops 16777216 | bytes 9568256 | tf_op jit(solution)/shard_map/convert.3
  185.3 7.4 %bitcast_dynamic-update-slice_fusion.2 = (f32[6,2048,128]{1,2,0:T(8,128)}, f32[2048,128]{0,1:T(8,128)S(1)}) fusion(f32[6,2048,128]{1,2,0:T(8,128)} %get-tuple-element.934, s32[]{:T(128)S(6)} %select_n.258, f32[128]{0:T(128)S(1)} %multiply_bitcast_fusion.2, bf16[1,128,2048]{2,1,0:T(8,128)(2,1)S(1)} %get-tuple-element.958, ...), kind=kOutput, calls=%fused_computation.8.clone.1 | convolution fusion | flops 1091043328 | bytes 11010564 | tf_op jit(solution)/shard_map/while/body/dot_general | solution.py:53
  194.9 1.3 dynamic_slice.163
  199.3 1.3 dynamic_slice.162
  201.5 4.8 %subtract_convert_fusion.4 = (bf16[16,128,1024]{2,1,0:T(8,128)(2,1)}, bf16[16,128,1024]{2,1,0:T(8,128)(2,1)}) fusion(f32[16,1024]{1,0:T(8,128)S(1)} %get-tuple-element.877, f32[128,1024]{1,0:T(8,128)S(1)} %get-tuple-element.878, f32[16,1024]{1,0:T(8,128)S(1)} %get-tuple-element.879, f32[128,1024]{1,0:T(8,128)S(1)} %get-tuple-element.880), kind=kLoop, calls=%fused_computation.5.clone.1 | loop fusion | flops 16777216 | bytes 9568256 | tf_op jit(solution)/shard_map/convert.3
  206.4 7.4 %bitcast_dynamic-update-slice_fusion.2 = (f32[6,2048,128]{1,2,0:T(8,128)}, f32[2048,128]{0,1:T(8,128)S(1)}) fusion(f32[6,2048,128]{1,2,0:T(8,128)} %get-tuple-element.934, s32[]{:T(128)S(6)} %select_n.258, f32[128]{0:T(128)S(1)} %multiply_bitcast_fusion.2, bf16[1,128,2048]{2,1,0:T(8,128)(2,1)S(1)} %get-tuple-element.958, ...), kind=kOutput, calls=%fused_computation.8.clone.1 | convolution fusion | flops 1091043328 | bytes 11010564 | tf_op jit(solution)/shard_map/while/body/dot_general | solution.py:53
  215.9 1.3 dynamic_slice.163
  220.3 1.3 dynamic_slice.162
  222.5 4.8 %subtract_convert_fusion.4 = (bf16[16,128,1024]{2,1,0:T(8,128)(2,1)}, bf16[16,128,1024]{2,1,0:T(8,128)(2,1)}) fusion(f32[16,1024]{1,0:T(8,128)S(1)} %get-tuple-element.877, f32[128,1024]{1,0:T(8,128)S(1)} %get-tuple-element.878, f32[16,1024]{1,0:T(8,128)S(1)} %get-tuple-element.879, f32[128,1024]{1,0:T(8,128)S(1)} %get-tuple-element.880), kind=kLoop, calls=%fused_computation.5.clone.1 | loop fusion | flops 16777216 | bytes 9568256 | tf_op jit(solution)/shard_map/convert.3
  227.4 7.4 %bitcast_dynamic-update-slice_fusion.2 = (f32[6,2048,128]{1,2,0:T(8,128)}, f32[2048,128]{0,1:T(8,128)S(1)}) fusion(f32[6,2048,128]{1,2,0:T(8,128)} %get-tuple-element.934, s32[]{:T(128)S(6)} %select_n.258, f32[128]{0:T(128)S(1)} %multiply_bitcast_fusion.2, bf16[1,128,2048]{2,1,0:T(8,128)(2,1)S(1)} %get-tuple-element.958, ...), kind=kOutput, calls=%fused_computation.8.clone.1 | convolution fusion | flops 1091043328 | bytes 11010564 | tf_op jit(solution)/shard_map/while/body/dot_general | solution.py:53
  236.9 1.3 dynamic_slice.163
  241.3 1.3 dynamic_slice.162
  243.6 4.8 %subtract_convert_fusion.4 = (bf16[16,128,1024]{2,1,0:T(8,128)(2,1)}, bf16[16,128,1024]{2,1,0:T(8,128)(2,1)}) fusion(f32[16,1024]{1,0:T(8,128)S(1)} %get-tuple-element.877, f32[128,1024]{1,0:T(8,128)S(1)} %get-tuple-element.878, f32[16,1024]{1,0:T(8,128)S(1)} %get-tuple-element.879, f32[128,1024]{1,0:T(8,128)S(1)} %get-tuple-element.880), kind=kLoop, calls=%fused_computation.5.clone.1 | loop fusion | flops 16777216 | bytes 9568256 | tf_op jit(solution)/shard_map/convert.3
  248.4 7.3 %bitcast_dynamic-update-slice_fusion.2 = (f32[6,2048,128]{1,2,0:T(8,128)}, f32[2048,128]{0,1:T(8,128)S(1)}) fusion(f32[6,2048,128]{1,2,0:T(8,128)} %get-tuple-element.934, s32[]{:T(128)S(6)} %select_n.258, f32[128]{0:T(128)S(1)} %multiply_bitcast_fusion.2, bf16[1,128,2048]{2,1,0:T(8,128)(2,1)S(1)} %get-tuple-element.958, ...), kind=kOutput, calls=%fused_computation.8.clone.1 | convolution fusion | flops 1091043328 | bytes 11010564 | tf_op jit(solution)/shard_map/while/body/dot_general | solution.py:53
  257.8 1.3 dynamic_slice.163
  262.3 1.3 dynamic_slice.162
  264.5 4.8 %subtract_convert_fusion.4 = (bf16[16,128,1024]{2,1,0:T(8,128)(2,1)}, bf16[16,128,1024]{2,1,0:T(8,128)(2,1)}) fusion(f32[16,1024]{1,0:T(8,128)S(1)} %get-tuple-element.877, f32[128,1024]{1,0:T(8,128)S(1)} %get-tuple-element.878, f32[16,1024]{1,0:T(8,128)S(1)} %get-tuple-element.879, f32[128,1024]{1,0:T(8,128)S(1)} %get-tuple-element.880), kind=kLoop, calls=%fused_computation.5.clone.1 | loop fusion | flops 16777216 | bytes 9568256 | tf_op jit(solution)/shard_map/convert.3
  269.4 7.4 %bitcast_dynamic-update-slice_fusion.2 = (f32[6,2048,128]{1,2,0:T(8,128)}, f32[2048,128]{0,1:T(8,128)S(1)}) fusion(f32[6,2048,128]{1,2,0:T(8,128)} %get-tuple-element.934, s32[]{:T(128)S(6)} %select_n.258, f32[128]{0:T(128)S(1)} %multiply_bitcast_fusion.2, bf16[1,128,2048]{2,1,0:T(8,128)(2,1)S(1)} %get-tuple-element.958, ...), kind=kOutput, calls=%fused_computation.8.clone.1 | convolution fusion | flops 1091043328 | bytes 11010564 | tf_op jit(solution)/shard_map/while/body/dot_general | solution.py:53
  277.7 16.7 %all-gather = f32[2048,8]{0,1:T(8,128)S(1)} all-gather(f32[128,8]{0,1:T(8,128)S(1)} %get-tuple-element.540), channel_id=2, replica_groups=mesh['grp'=2,'orient'=16] {'orient'}, dimensions={0}, use_global_device_ids=true | all-gather | bytes 69632 | tf_op jit(solution)/shard_map/all_gather | solution.py:15
  294.4 19.8 %all-gather.1 = f32[2048,8]{0,1:T(8,128)S(1)} all-gather(f32[128,8]{0,1:T(8,128)S(1)} %get-tuple-element.541), channel_id=3, replica_groups=mesh['grp'=2,'orient'=16] {'orient'}, dimensions={0}, use_global_device_ids=true | all-gather | bytes 69632 | tf_op jit(solution)/shard_map/all_gather | solution.py:15
  315.1 122.0 %while.51 = (s32[]{:T(128)}, f32[1,128,2048]{2,1,0:T(8,128)S(1)}, f32[1,128]{1,0:T(1,128)S(1)}, s32[]{:T(128)}, f32[6,2048,128]{1,2,0:T(8,128)}, /*index=5*/s32[...) while((s32[]{:T(128)}, f32[1,128,2048]{2,1,0:T(8,128)S(1)}, ...), condition=%wide.region_11.12_spmd, body=%wide.region_9.11_spmd.sunk | while | flops 1109998848 | bytes 29153852 | solution.py:157
  317.1 1.3 dynamic_slice.169
  321.5 1.3 dynamic_slice.168
  323.8 4.8 %subtract_convert_fusion.5 = (bf16[16,128,1024]{2,1,0:T(8,128)(2,1)}, bf16[16,128,1024]{2,1,0:T(8,128)(2,1)}) fusion(f32[16,1024]{1,0:T(8,128)S(1)} %get-tuple-element.909, f32[128,1024]{1,0:T(8,128)S(1)} %get-tuple-element.910, f32[16,1024]{1,0:T(8,128)S(1)} %get-tuple-element.911, f32[128,1024]{1,0:T(8,128)S(1)} %get-tuple-element.912), kind=kLoop, calls=%fused_computation.57.clone.1 | loop fusion | flops 16777216 | bytes 9568256 | tf_op jit(solution)/shard_map/convert.4
  328.6 1.3 constant_dynamic-slice_fusion.6
  330.2 4.5 %fusion.84 = f32[1,128,2048]{2,1,0:T(8,128)S(1)} fusion(bf16[16,128,1024]{2,1,0:T(8,128)(2,1)} %get-tuple-element.913, bf16[16,128,1024]{2,1,0:T(8,128)(2,1)} %get-tuple-element.914, f32[1,128,2048]{2,1,0:T(8,128)S(1)} %get-tuple-element.1005, f32[16,128,128]{2,1,0:T(8,128)S(1)} %bitcast.141, f32[128]{0:T(128)S(1)} %get-tuple-element.915, ...), kind=kOutput, calls=%fused_computation.60.clone.1 | convolution fusion | flops 1091567616 | bytes 11535360 | tf_op jit(solution)/shard_map/while/body/dot_general | solution.py:140
  337.3 1.3 dynamic_slice.169
  341.7 1.3 dynamic_slice.168
  344.0 4.8 %subtract_convert_fusion.5 = (bf16[16,128,1024]{2,1,0:T(8,128)(2,1)}, bf16[16,128,1024]{2,1,0:T(8,128)(2,1)}) fusion(f32[16,1024]{1,0:T(8,128)S(1)} %get-tuple-element.909, f32[128,1024]{1,0:T(8,128)S(1)} %get-tuple-element.910, f32[16,1024]{1,0:T(8,128)S(1)} %get-tuple-element.911, f32[128,1024]{1,0:T(8,128)S(1)} %get-tuple-element.912), kind=kLoop, calls=%fused_computation.57.clone.1 | loop fusion | flops 16777216 | bytes 9568256 | tf_op jit(solution)/shard_map/convert.4
  348.8 1.3 constant_dynamic-slice_fusion.6
  350.4 4.5 %fusion.84 = f32[1,128,2048]{2,1,0:T(8,128)S(1)} fusion(bf16[16,128,1024]{2,1,0:T(8,128)(2,1)} %get-tuple-element.913, bf16[16,128,1024]{2,1,0:T(8,128)(2,1)} %get-tuple-element.914, f32[1,128,2048]{2,1,0:T(8,128)S(1)} %get-tuple-element.1005, f32[16,128,128]{2,1,0:T(8,128)S(1)} %bitcast.141, f32[128]{0:T(128)S(1)} %get-tuple-element.915, ...), kind=kOutput, calls=%fused_computation.60.clone.1 | convolution fusion | flops 1091567616 | bytes 11535360 | tf_op jit(solution)/shard_map/while/body/dot_general | solution.py:140
  357.5 1.3 dynamic_slice.169
  361.9 1.3 dynamic_slice.168
  364.2 4.8 %subtract_convert_fusion.5 = (bf16[16,128,1024]{2,1,0:T(8,128)(2,1)}, bf16[16,128,1024]{2,1,0:T(8,128)(2,1)}) fusion(f32[16,1024]{1,0:T(8,128)S(1)} %get-tuple-element.909, f32[128,1024]{1,0:T(8,128)S(1)} %get-tuple-element.910, f32[16,1024]{1,0:T(8,128)S(1)} %get-tuple-element.911, f32[128,1024]{1,0:T(8,128)S(1)} %get-tuple-element.912), kind=kLoop, calls=%fused_computation.57.clone.1 | loop fusion | flops 16777216 | bytes 9568256 | tf_op jit(solution)/shard_map/convert.4
  369.0 1.3 constant_dynamic-slice_fusion.6
  370.6 4.5 %fusion.84 = f32[1,128,2048]{2,1,0:T(8,128)S(1)} fusion(bf16[16,128,1024]{2,1,0:T(8,128)(2,1)} %get-tuple-element.913, bf16[16,128,1024]{2,1,0:T(8,128)(2,1)} %get-tuple-element.914, f32[1,128,2048]{2,1,0:T(8,128)S(1)} %get-tuple-element.1005, f32[16,128,128]{2,1,0:T(8,128)S(1)} %bitcast.141, f32[128]{0:T(128)S(1)} %get-tuple-element.915, ...), kind=kOutput, calls=%fused_computation.60.clone.1 | convolution fusion | flops 1091567616 | bytes 11535360 | tf_op jit(solution)/shard_map/while/body/dot_general | solution.py:140
  377.7 1.3 dynamic_slice.169
  382.1 1.3 dynamic_slice.168
  384.4 4.8 %subtract_convert_fusion.5 = (bf16[16,128,1024]{2,1,0:T(8,128)(2,1)}, bf16[16,128,1024]{2,1,0:T(8,128)(2,1)}) fusion(f32[16,1024]{1,0:T(8,128)S(1)} %get-tuple-element.909, f32[128,1024]{1,0:T(8,128)S(1)} %get-tuple-element.910, f32[16,1024]{1,0:T(8,128)S(1)} %get-tuple-element.911, f32[128,1024]{1,0:T(8,128)S(1)} %get-tuple-element.912), kind=kLoop, calls=%fused_computation.57.clone.1 | loop fusion | flops 16777216 | bytes 9568256 | tf_op jit(solution)/shard_map/convert.4
  389.2 1.3 constant_dynamic-slice_fusion.6
  390.8 4.5 %fusion.84 = f32[1,128,2048]{2,1,0:T(8,128)S(1)} fusion(bf16[16,128,1024]{2,1,0:T(8,128)(2,1)} %get-tuple-element.913, bf16[16,128,1024]{2,1,0:T(8,128)(2,1)} %get-tuple-element.914, f32[1,128,2048]{2,1,0:T(8,128)S(1)} %get-tuple-element.1005, f32[16,128,128]{2,1,0:T(8,128)S(1)} %bitcast.141, f32[128]{0:T(128)S(1)} %get-tuple-element.915, ...), kind=kOutput, calls=%fused_computation.60.clone.1 | convolution fusion | flops 1091567616 | bytes 11535360 | tf_op jit(solution)/shard_map/while/body/dot_general | solution.py:140
  397.9 1.3 dynamic_slice.169
  404.6 4.8 %subtract_convert_fusion.5 = (bf16[16,128,1024]{2,1,0:T(8,128)(2,1)}, bf16[16,128,1024]{2,1,0:T(8,128)(2,1)}) fusion(f32[16,1024]{1,0:T(8,128)S(1)} %get-tuple-element.909, f32[128,1024]{1,0:T(8,128)S(1)} %get-tuple-element.910, f32[16,1024]{1,0:T(8,128)S(1)} %get-tuple-element.911, f32[128,1024]{1,0:T(8,128)S(1)} %get-tuple-element.912), kind=kLoop, calls=%fused_computation.57.clone.1 | loop fusion | flops 16777216 | bytes 9568256 | tf_op jit(solution)/shard_map/convert.4
  409.4 1.3 constant_dynamic-slice_fusion.6
  411.0 4.5 %fusion.84 = f32[1,128,2048]{2,1,0:T(8,128)S(1)} fusion(bf16[16,128,1024]{2,1,0:T(8,128)(2,1)} %get-tuple-element.913, bf16[16,128,1024]{2,1,0:T(8,128)(2,1)} %get-tuple-element.914, f32[1,128,2048]{2,1,0:T(8,128)S(1)} %get-tuple-element.1005, f32[16,128,128]{2,1,0:T(8,128)S(1)} %bitcast.141, f32[128]{0:T(128)S(1)} %get-tuple-element.915, ...), kind=kOutput, calls=%fused_computation.60.clone.1 | convolution fusion | flops 1091567616 | bytes 11535360 | tf_op jit(solution)/shard_map/while/body/dot_general | solution.py:140
  424.8 4.8 %subtract_convert_fusion.5 = (bf16[16,128,1024]{2,1,0:T(8,128)(2,1)}, bf16[16,128,1024]{2,1,0:T(8,128)(2,1)}) fusion(f32[16,1024]{1,0:T(8,128)S(1)} %get-tuple-element.909, f32[128,1024]{1,0:T(8,128)S(1)} %get-tuple-element.910, f32[16,1024]{1,0:T(8,128)S(1)} %get-tuple-element.911, f32[128,1024]{1,0:T(8,128)S(1)} %get-tuple-element.912), kind=kLoop, calls=%fused_computation.57.clone.1 | loop fusion | flops 16777216 | bytes 9568256 | tf_op jit(solution)/shard_map/convert.4
  429.6 1.3 constant_dynamic-slice_fusion.6
  431.2 4.5 %fusion.84 = f32[1,128,2048]{2,1,0:T(8,128)S(1)} fusion(bf16[16,128,1024]{2,1,0:T(8,128)(2,1)} %get-tuple-element.913, bf16[16,128,1024]{2,1,0:T(8,128)(2,1)} %get-tuple-element.914, f32[1,128,2048]{2,1,0:T(8,128)S(1)} %get-tuple-element.1005, f32[16,128,128]{2,1,0:T(8,128)S(1)} %bitcast.141, f32[128]{0:T(128)S(1)} %get-tuple-element.915, ...), kind=kOutput, calls=%fused_computation.60.clone.1 | convolution fusion | flops 1091567616 | bytes 11535360 | tf_op jit(solution)/shard_map/while/body/dot_general | solution.py:140
  (218 shorter events, 49.2 us)
Async XLA Ops:
  0.6 141.8 %copy-start.2 = (bf16[64,2048]{1,0:T(8,128)(2,1)S(1)}, bf16[64,2048]{1,0:T(8,128)(2,1)}, u32[]{:S(2)}) copy-start(bf16[64,2048]{1,0:T(8,128)(2,1)} %param.11) | copy-start | bytes 786436
  0.6 4.3 collective-permute-start
  4.9 42.2 %copy-start.3 = (bf16[64,2048]{1,0:T(8,128)(2,1)}, bf16[64,2048]{1,0:T(8,128)(2,1)S(1)}, u32[]{:S(2)}) copy-start(bf16[64,2048]{1,0:T(8,128)(2,1)S(1)} %collective-permute-done) | copy-start | bytes 786436
  6.0 14.2 %collective-permute-start.1 = (bf16[128,2048]{1,0:T(8,128)(2,1)S(1)}, bf16[128,2048]{1,0:T(8,128)(2,1)S(1)}, u32[]{:S(2)}, u32[]{:S(2)}) collective-permute-start(bf16[128,2048]{1,0:T(8,128)(2,1)S(1)} %pad_maximum_fusion.2), channel_id=1, source_target_pairs={{0,14},{1,15},{2,0},{3,1},{4,2},{5,3},{6,4},{7,5},{8,6},{9,7},{10,... | collective-permute-start | bytes 1572872 | tf_op jit(solution)/shard_map/ppermute | solution.py:82
  20.2 26.9 %copy-start = (bf16[128,2048]{1,0:T(8,128)(2,1)}, bf16[128,2048]{1,0:T(8,128)(2,1)S(1)}, u32[]{:S(2)}) copy-start(bf16[128,2048]{1,0:T(8,128)(2,1)S(1)} %collective-permute-done.1) | copy-start | bytes 1572868
  21.4 25.7 %collective-permute-start.2 = (bf16[256,2048]{1,0:T(8,128)(2,1)S(1)}, bf16[256,2048]{1,0:T(8,128)(2,1)S(1)}, u32[]{:S(2)}, u32[]{:S(2)}) collective-permute-start(bf16[256,2048]{1,0:T(8,128)(2,1)S(1)} %pad_maximum_fusion.1), channel_id=1, source_target_pairs={{0,12},{1,13},{2,14},{3,15},{4,0},{5,1},{6,2},{7,3},{8,4},{9,5},{1... | collective-permute-start | bytes 3145736 | tf_op jit(solution)/shard_map/ppermute | solution.py:82
  49.5 92.7 %collective-permute-start.3 = (bf16[512,2048]{1,0:T(8,128)(2,1)}, bf16[512,2048]{1,0:T(8,128)(2,1)S(1)}, u32[]{:S(2)}, u32[]{:S(2)}) collective-permute-start(bf16[512,2048]{1,0:T(8,128)(2,1)} %pad_maximum_fusion), channel_id=1, source_target_pairs={{0,8},{1,9},{2,10},{3,11},{4,12},{5,13},{6,14},{7,15},{8,0},{9,1},... | collective-permute-start | bytes 6291464 | tf_op jit(solution)/shard_map/ppermute | solution.py:82
  49.9 92.6 %copy-start.4 = (bf16[64,2048]{1,0:T(8,128)(2,1)S(1)}, bf16[64,2048]{1,0:T(8,128)(2,1)}, u32[]{:S(2)}) copy-start(bf16[64,2048]{1,0:T(8,128)(2,1)} %copy-done.3) | copy-start | bytes 786436
  49.9 92.6 %copy-start.1 = (bf16[128,2048]{1,0:T(8,128)(2,1)S(1)}, bf16[128,2048]{1,0:T(8,128)(2,1)}, u32[]{:S(2)}) copy-start(bf16[128,2048]{1,0:T(8,128)(2,1)} %copy-done) | copy-start | bytes 1572868
  143.3 7.8 %copy-start.6 = (bf16[128,2048]{1,0:T(8,128)(2,1)S(1)}, bf16[128,2048]{1,0:T(8,128)(2,1)}, u32[]{:S(2)}) copy-start(bf16[128,2048]{1,0:T(8,128)(2,1)} %param.12) | copy-start | bytes 1572868
  437.2 1.0 copy-start.5
  437.2 1.0 copy-start.7
